TPU v7x, 512 devices: a whole 4x8x8 slice. The times are simulated.
512 devices in a mesh: head: 8 (over x, core), blk: 64 (over y, z).
Axes of the slice: x: 4, y: 8, z: 8, core: 2. Of those that a mesh axis runs over, the one named last changes fastest.
Arguments:
- suffix_hidden: bfloat16 [1536, 2048], P('blk'), may hold values from -400 to 400
- prefix_hidden: bfloat16 [16384, 2048], P('blk'), may hold values from -400 to 400
- kv_cache: bfloat16 [2, 16384, 8, 256], P(None, 'blk', 'head'), may hold values from -300 to 300
- norm_gain: float32 [2048], replicated, may hold values from 0.1 to 1.9
- norm_bias: float32 [2048], replicated, may hold values from -3 to 3
- qkv_weight: bfloat16 [2048, 8, 768], P('blk', 'head'), may hold values from -0.125 to 0.125
- qkv_bias: float32 [8, 768], P('head'), may hold values from -3 to 3
- out_weight: bfloat16 [8, 256, 2048], P('head', 'blk'), may hold values from -0.125 to 0.125
- out_bias: float32 [2048], replicated, may hold values from -3 to 3
- suffix_lengths: int32 [4], replicated, may hold values from 1 to 768, 1536 in all
- prefix_blocks: int32 [4], replicated, may hold values from 1 to 32, 64 in all
- block_owner: int32 [64], replicated, may hold values from 0 to 63, each once
- recompute_flag: int32 [16384], P('blk'), may hold values from 0 to 1, as said below
Outputs:
- attn_out: bfloat16 [1536, 2048], P('blk', 'head')
Inputs may be any that keep to these rules, and one draw needn't show every extreme that they name: `recompute_flag`: each storage block of 256 cache rows holds exactly 25 ones.
All inputs are finite; a program needn't handle non-finite values.
Results may differ from a plain program's by a relative error of at most 0.015.
Values may be sent and summed in bfloat16 or wider, within the bound.
A program may use at most 64 MiB of HBM per device.

v0:
```python
import math
import jax
import jax.numpy as jnp
from jax import lax
from jax.sharding import PartitionSpec as P

FLAG_DEV = 25
EPSILON = 1e-05
MASKED = -1e30


def layer_norm(states, norm_scale, norm_shift):
    widened = states.astype(jnp.float32)
    average = jnp.mean(widened, axis=-1, keepdims=True)
    center = widened - average
    variance = jnp.mean(center * center, axis=-1, keepdims=True)
    return (center * lax.rsqrt(variance + EPSILON) * norm_scale + norm_shift).astype(jnp.bfloat16)


def body(
    suffix_hidden,
    prefix_hidden,
    kv_cache,
    norm_gain,
    norm_bias,
    qkv_weight,
    qkv_bias,
    out_weight,
    out_bias,
    suffix_lengths,
    prefix_blocks,
    block_owner,
    recompute_flag,
):
    blk_total = lax.axis_size("blk")
    own_index = lax.axis_index("blk")
    row_count = suffix_hidden.shape[0]
    cache_rows = prefix_hidden.shape[0]
    heads_dev = qkv_weight.shape[1]
    head_dim = qkv_weight.shape[2] // 3
    total_rows = row_count * blk_total
    own_first = own_index * row_count
    tenant_ends = jnp.cumsum(suffix_lengths)
    row_ids = jnp.arange(total_rows, dtype=jnp.int32)
    row_tenant = jnp.sum((row_ids[:, None] >= tenant_ends[None, :]).astype(jnp.int32), axis=1)
    block_ends = jnp.cumsum(prefix_blocks)
    block_slots = jnp.arange(blk_total, dtype=jnp.int32)
    global_block = jnp.sum(jnp.where(block_owner == own_index, block_slots, 0))
    block_tenant = jnp.sum((global_block >= block_ends).astype(jnp.int32))
    normed = layer_norm(suffix_hidden, norm_gain, norm_bias)
    flagged = jnp.argsort(1 - recompute_flag, stable=True)[:FLAG_DEV]
    prefix_normed = layer_norm(prefix_hidden[flagged], norm_gain, norm_bias)
    qkv_rows = qkv_weight.shape[0]
    out_rows = out_weight.shape[1]
    model_dim = out_weight.shape[2]
    packed_weights = jnp.concatenate([qkv_weight.reshape(1, -1), out_weight.reshape(1, -1)], axis=1)
    fetched_all = lax.all_gather(packed_weights, "blk", axis=0, tiled=True)
    qkv_size = qkv_rows * heads_dev * 3 * head_dim
    fetched = fetched_all[:, :qkv_size].reshape(blk_total * qkv_rows, heads_dev, 3 * head_dim)
    out_fetched = fetched_all[:, qkv_size:].reshape(blk_total, heads_dev, out_rows, model_dim)
    out_fetched = jnp.transpose(out_fetched, (1, 0, 2, 3)).reshape(
        heads_dev, blk_total * out_rows, model_dim
    )
    piece_rows = fetched.shape[0]
    flattened = fetched.reshape(piece_rows, heads_dev * 3 * head_dim)
    kv_part = fetched[:, :, head_dim:].reshape(piece_rows, heads_dev * 2 * head_dim)
    suffix_acc = jnp.dot(normed, flattened, preferred_element_type=jnp.float32)
    prefix_acc = jnp.dot(prefix_normed, kv_part, preferred_element_type=jnp.float32)
    suffix_acc, prefix_acc = (suffix_acc, prefix_acc)
    projected = (
        (suffix_acc + qkv_bias.reshape(-1))
        .astype(jnp.bfloat16)
        .reshape(row_count, heads_dev, 3 * head_dim)
    )
    recomputed = (
        (prefix_acc + qkv_bias[:, head_dim:].reshape(-1))
        .astype(jnp.bfloat16)
        .reshape(FLAG_DEV, heads_dev, 2 * head_dim)
    )
    own_queries = projected[:, :, :head_dim].reshape(row_count, heads_dev * head_dim)
    gathered = lax.all_gather(own_queries, "blk", axis=0, tiled=True)
    prefix_keys = kv_cache[0].at[flagged].set(recomputed[:, :, :head_dim])
    prefix_values = kv_cache[1].at[flagged].set(recomputed[:, :, head_dim:])
    keys_all = jnp.concatenate([prefix_keys, projected[:, :, head_dim : 2 * head_dim]], axis=0)
    values_all = jnp.concatenate([prefix_values, projected[:, :, 2 * head_dim :]], axis=0)
    own_tenant = lax.dynamic_slice_in_dim(row_tenant, own_first, row_count, 0)
    key_tenant = jnp.concatenate([jnp.full((cache_rows,), block_tenant, jnp.int32), own_tenant])
    key_position = jnp.concatenate(
        [jnp.full((cache_rows,), -1, jnp.int32), own_first + jnp.arange(row_count, dtype=jnp.int32)]
    )
    scale = head_dim ** (-0.5)
    qblock = math.gcd(total_rows, 512)
    block_total = total_rows // qblock

    def partial_block(offset):
        query_block = lax.dynamic_slice_in_dim(gathered, offset, qblock, 0).reshape(
            qblock, heads_dev, head_dim
        )
        query_tenant = lax.dynamic_slice_in_dim(row_tenant, offset, qblock, 0)
        query_position = offset + jnp.arange(qblock, dtype=jnp.int32)
        allowed = (query_tenant[:, None] == key_tenant[None, :]) & (
            key_position[None, :] <= query_position[:, None]
        )
        scores = (
            jnp.einsum("qhd,khd->hqk", query_block, keys_all, preferred_element_type=jnp.float32)
            * scale
        )
        gate = allowed[None, :, :]
        row_peak = jnp.max(jnp.where(gate, scores, MASKED), axis=2)
        weights = jnp.where(gate, jnp.exp(scores - row_peak[:, :, None]), 0.0)
        denominator = jnp.sum(weights, axis=2)
        numerator = jnp.einsum(
            "hqk,khd->qhd",
            weights.astype(jnp.bfloat16),
            values_all,
            preferred_element_type=jnp.float32,
        )
        return (numerator.reshape(qblock, heads_dev * head_dim), denominator.T, row_peak.T)

    def fill_block(step_index, buffers):
        numer_buf, denom_buf, peak_buf = buffers
        offset = step_index * qblock
        numerator, denominator, row_peak = partial_block(offset)
        numer_buf = lax.dynamic_update_slice_in_dim(numer_buf, numerator, offset, 0)
        denom_buf = lax.dynamic_update_slice_in_dim(denom_buf, denominator, offset, 0)
        peak_buf = lax.dynamic_update_slice_in_dim(peak_buf, row_peak, offset, 0)
        return (numer_buf, denom_buf, peak_buf)

    initial = (
        jnp.zeros((total_rows, heads_dev * head_dim), jnp.float32),
        jnp.zeros((total_rows, heads_dev), jnp.float32),
        jnp.full((total_rows, heads_dev), MASKED, jnp.float32),
    )
    numer_buf, denom_buf, peak_buf = lax.fori_loop(0, block_total, fill_block, initial)
    width = heads_dev * head_dim + 2 * heads_dev
    packed = jnp.concatenate([numer_buf, denom_buf, peak_buf], axis=1).reshape(
        blk_total, row_count * width
    )
    received = lax.all_to_all(packed, "blk", split_axis=0, concat_axis=0, tiled=True)
    received = received.reshape(blk_total, row_count, width)
    recv_numer = received[:, :, : heads_dev * head_dim]
    recv_denom = received[:, :, heads_dev * head_dim : heads_dev * head_dim + heads_dev]
    recv_peak = received[:, :, heads_dev * head_dim + heads_dev :]
    best = jnp.max(recv_peak, axis=0)
    factor = jnp.exp(recv_peak - best[None])
    summed_denom = jnp.sum(factor * recv_denom, axis=0)
    summed_numer = jnp.sum(
        recv_numer.reshape(blk_total, row_count, heads_dev, head_dim) * factor[:, :, :, None],
        axis=0,
    )
    attended = (summed_numer / summed_denom[:, :, None]).astype(jnp.bfloat16)
    mixed = jnp.einsum("rhd,hde->re", attended, out_fetched, preferred_element_type=jnp.float32)
    head_total = lax.axis_size("head")
    columns = mixed.shape[1] // head_total
    pieces = mixed.astype(jnp.bfloat16).reshape(row_count, head_total, columns)
    pieces = jnp.transpose(pieces, (1, 0, 2))
    exchanged = lax.all_to_all(pieces, "head", split_axis=0, concat_axis=0, tiled=True)
    summed = jnp.sum(exchanged.astype(jnp.float32), axis=0)
    bias_part = lax.dynamic_slice_in_dim(out_bias, lax.axis_index("head") * columns, columns, 0)
    return (summed + bias_part).astype(jnp.bfloat16)


def solution(mesh):
    return jax.shard_map(
        body,
        mesh=mesh,
        in_specs=(
            P("blk", None),
            P("blk", None),
            P(None, "blk", "head", None),
            P(),
            P(),
            P("blk", "head", None),
            P("head", None),
            P("head", "blk", None),
            P(),
            P(),
            P(),
            P(),
            P("blk"),
        ),
        out_specs=P("blk", "head"),
        check_vma=False,
    )
```

profile of v0, /device:TPU:8, one launch (start us, length us, event | category | flops | bytes accessed | tf_op | source)
XLA Modules:
  0.0 287.5 jit_solution(16090769834102768445)
XLA Ops:
  16.3 3.2 %sort.17 = (s32[256]{0:T(256)}, s32[256]{0:T(256)S(1)}) sort(s32[256]{0:T(256)S(1)} %broadcast_subtract_fusion, s32[256]{0:T(256)S(1)} %iota.25), dimensions={0}, to_apply=%region_7.8 | sort | flops 2048 | bytes 4096 | tf_op jit(solution)/shard_map/jit(argsort)/sort | solution.py:51
  22.6 91.7 %all-gather.4.cloned.1.call-done = bf16[64,1,32768]{2,1,0:T(2,128)(2,1)} async-done(((bf16[1,1,32768]{2,1,0:T(2,128)(2,1)}), bf16[64,1,32768]{2,1,0:T(2,128)(2,1)}) %all-gather.4.cloned.1.call-update) | async-done | bytes 4194320 | tf_op jit(solution)/shard_map/all_gather | solution.py:57
  114.3 7.9 %copy.55 = bf16[64,1,32768]{2,0,1:T(8,128)(2,1)S(1)} copy(bf16[64,1,32768]{2,1,0:T(2,128)(2,1)} %all-gather.4.cloned.1.call-done) | data formatting | bytes 8388608
  122.2 1.9 copy-done.1
  124.2 1.9 slice.62
  126.0 4.8 %reshape_reshape.3 = bf16[2048,768]{1,0:T(8,128)(2,1)} reshape(bf16[64,24576]{1,0:T(8,128)(2,1)} %slice.62) | data formatting | bytes 6291456 | tf_op jit(solution)/shard_map/reshape;reshape | solution.py:65
  130.9 4.9 %reshape.221 = bf16[2048,1,768]{2,0,1:T(8,128)(2,1)} reshape(bf16[64,24576]{1,0:T(8,128)(2,1)} %slice.62) | data formatting | bytes 6291456 | tf_op jit(solution)/shard_map/reshape | solution.py:59
  135.8 2.6 fusion.19
  138.5 49.4 %all-gather = bf16[1536,1,256]{2,0,1:T(8,128)(2,1)S(1)} all-gather(bf16[24,1,256]{2,0,1:T(8,128)(2,1)S(1)} %get-tuple-element.212), channel_id=2, replica_groups=mesh['head'=8,'blk'=64] {'blk'}, dimensions={0}, use_global_device_ids=true | all-gather | bytes 798720 | tf_op jit(solution)/shard_map/all_gather | solution.py:81
  192.1 11.9 %while.17 = (s32[]{:T(128)}, f32[1536,256]{1,0:T(8,128)S(1)}, f32[1536,1]{0,1:T(1,128)}, f32[1536,1]{0,1:T(1,128)}, s32[1536]{0:T(1024)}, /*index=5*/s32[280]{0:...) while((s32[]{:T(128)}, f32[1536,256]{1,0:T(8,128)S(1)}, ...), condition=%wide.region_15.16_spmd, body=%wide.region_12.15_spmd.sunk | while | flops 149380608 | bytes 2841579 | solution.py:134
  204.0 1.9 copy.40
  205.9 1.9 copy.39
  207.8 2.2 pad_maximum_fusion
  210.0 4.3 %all_to_all.12 = f32[64,1,6192]{2,1,0:T(1,128)} reshape(f32[1536,258]{1,0:T(8,128)S(1)} %pad_maximum_fusion) | data formatting | bytes 3170304 | tf_op jit(solution)/shard_map/all_to_all | solution.py:139
  214.3 10.0 %all-to-all-start = ((f32[64,1,6192]{2,1,0:T(1,128)}), f32[64,1,6192]{2,1,0:T(1,128)S(1)}, u32[]{:S(2)}, u32[]{:S(2)}) async-start(f32[64,1,6192]{2,1,0:T(1,128)} %all_to_all.12), calls=%async_computation | async-start | bytes 3211264 | tf_op jit(solution)/shard_map/all_to_all | solution.py:139
  224.3 2.3 slice.72
  226.6 2.7 reshape.225
  229.3 25.7 %all-to-all-done = f32[64,1,6192]{2,1,0:T(1,128)S(1)} async-done(((f32[64,1,6192]{2,1,0:T(1,128)}), f32[64,1,6192]{2,1,0:T(1,128)S(1)}, u32[]{:S(2)}, u32[]{:S(2)}) %all-to-all-start) | async-done | bytes 1585184 | tf_op jit(solution)/shard_map/all_to_all | solution.py:139
  255.0 5.4 %reduce.14 = f32[64,6192]{1,0:T(8,128)} reduce(f32[64,1,6192]{2,1,0:T(1,128)S(1)} %all-to-all-done, f32[]{:T(128)} %constant.108), dimensions={1}, to_apply=%all_to_all.10.reduce_sub_computation | reduce | bytes 3170308 | tf_op jit(solution)/shard_map/all_to_all | solution.py:139
  260.4 2.5 reshape.224
  262.9 1.5 fusion.51
  267.8 1.5 convolution_convert_fusion
  270.0 4.3 %all-to-all-start.1 = ((bf16[8,24,256]{2,1,0:T(8,128)(2,1)}), bf16[8,24,256]{2,1,0:T(8,128)(2,1)S(1)}, u32[]{:S(2)}, u32[]{:S(2)}) async-start(bf16[8,24,256]{2,1,0:T(8,128)(2,1)} %bitcast.70), calls=%async_computation.1 | async-start | bytes 196608 | tf_op jit(solution)/shard_map/all_to_all | solution.py:157
  275.0 5.0 %all-to-all-done.1 = bf16[8,24,256]{2,1,0:T(8,128)(2,1)S(1)} async-done(((bf16[8,24,256]{2,1,0:T(8,128)(2,1)}), bf16[8,24,256]{2,1,0:T(8,128)(2,1)S(1)}, u32[]{:S(2)}, u32[]{:S(2)}) %all-to-all-start.1) | async-done | bytes 98336 | tf_op jit(solution)/shard_map/all_to_all | solution.py:157
  (89 shorter events, 34.4 us)
Async XLA Ops:
  6.5 12.9 %copy-start = (bf16[256,2048]{1,0:T(8,128)(2,1)S(1)}, bf16[256,2048]{1,0:T(8,128)(2,1)}, u32[]{:S(2)}) copy-start(bf16[256,2048]{1,0:T(8,128)(2,1)} %param.16) | copy-start | bytes 3145732
  6.5 16.1 %copy-start.5 = (bf16[2,256,1,256]{3,1,2,0:T(8,128)(2,1)S(1)}, bf16[2,256,1,256]{3,1,2,0:T(8,128)(2,1)}, u32[]{:S(2)}) copy-start(bf16[2,256,1,256]{3,1,2,0:T(8,128)(2,1)} %param.17) | copy-start | bytes 786436
  6.5 107.8 %all-gather.4.cloned.1.call-start = ((), (), s32[]{:S(2)}) async-start(), calls=%async_computation.2 | async-start | bytes 8519680 | tf_op jit(solution)/shard_map/all_gather | solution.py:57
  11.5 1.5 copy-start.7
  122.2 1.9 copy-start.1
  130.9 4.9 %copy-start.4 = (bf16[24,2048]{1,0:T(8,128)(2,1)S(1)}, bf16[24,2048]{1,0:T(8,128)(2,1)}, u32[]{:S(2)}) copy-start(bf16[24,2048]{1,0:T(8,128)(2,1)} %param.15) | copy-start | bytes 294916
  130.9 4.9 %copy-start.8 = (f32[2048]{0:T(1024)S(1)}, f32[2048]{0:T(1024)}, u32[]{:S(2)}) copy-start(f32[2048]{0:T(1024)} %param.19) | copy-start | bytes 24580
  130.9 4.9 %copy-start.9 = (f32[2048]{0:T(1024)S(1)}, f32[2048]{0:T(1024)}, u32[]{:S(2)}) copy-start(f32[2048]{0:T(1024)} %param.18) | copy-start | bytes 24580
  135.8 52.0 %copy-start.3 = (bf16[2048,1,768]{2,0,1:T(8,128)(2,1)S(1)}, bf16[2048,1,768]{2,0,1:T(8,128)(2,1)}, u32[]{:S(2)}) copy-start(bf16[2048,1,768]{2,0,1:T(8,128)(2,1)} %reshape.221) | copy-start | bytes 9437188
  135.8 52.0 %slice-start = ((f32[1,768]{1,0:T(1,128)}), f32[1,512]{1,0:T(1,128)S(1)}, s32[]{:S(2)}) async-start(f32[1,768]{1,0:T(1,128)} %param.21), calls=%async_computation.3 | async-start | bytes 4096 | tf_op jit(solution)/shard_map/slice | solution.py:76
  192.1 3.1 %copy-start.6 = (s32[280]{0:T(512)S(1)}, s32[280]{0:T(512)}, u32[]{:S(2)}) copy-start(s32[280]{0:T(512)} %get-tuple-element.320) | copy-start | bytes 3364 | tf_op jit(solution)/shard_map/while
  196.1 3.1 %copy-start.6 = (s32[280]{0:T(512)S(1)}, s32[280]{0:T(512)}, u32[]{:S(2)}) copy-start(s32[280]{0:T(512)} %get-tuple-element.320) | copy-start | bytes 3364 | tf_op jit(solution)/shard_map/while
  200.0 3.2 %copy-start.6 = (s32[280]{0:T(512)S(1)}, s32[280]{0:T(512)}, u32[]{:S(2)}) copy-start(s32[280]{0:T(512)} %get-tuple-element.320) | copy-start | bytes 3364 | tf_op jit(solution)/shard_map/while
  204.0 3.8 %copy-start.2 = (f32[1536,256]{1,0:T(8,128)}, f32[1536,256]{1,0:T(8,128)S(1)}, u32[]{:S(2)}) copy-start(f32[1536,256]{1,0:T(8,128)S(1)} %get-tuple-element.178) | copy-start | bytes 4718596
  214.3 40.7 %all-to-all-start = ((f32[64,1,6192]{2,1,0:T(1,128)}), f32[64,1,6192]{2,1,0:T(1,128)S(1)}, u32[]{:S(2)}, u32[]{:S(2)}) async-start(f32[64,1,6192]{2,1,0:T(1,128)} %all_to_all.12), calls=%async_computation | async-start | bytes 3211264 | tf_op jit(solution)/shard_map/all_to_all | solution.py:139
  270.0 10.1 %all-to-all-start.1 = ((bf16[8,24,256]{2,1,0:T(8,128)(2,1)}), bf16[8,24,256]{2,1,0:T(8,128)(2,1)S(1)}, u32[]{:S(2)}, u32[]{:S(2)}) async-start(bf16[8,24,256]{2,1,0:T(8,128)(2,1)} %bitcast.70), calls=%async_computation.1 | async-start | bytes 196608 | tf_op jit(solution)/shard_map/all_to_all | solution.py:157
Sparse Core Ops, SparseCore 0:
  10.4 103.9 all-gather.3
where the time goes:
time: 289 us; the launch traced here: 288 us
  waiting for transfers between devices  122 us (42%)
  local copies, waits for them, and re-layouts  52.2 us (18%)
  blocking collectives  49.4 us (17%)
  other arithmetic  23.7 us (8%)
  starting transfers between devices  14.3 us (5%)
  between operations  13.6 us (5%)
  matrix products  11.7 us (4%)
    all_gather x1, waiting for transfers between devices, body(): fetched_all = lax.all_gather(packed_weights, 'blk', axis=0, tiled=True)  91.7 us
    all_gather x1, blocking collectives, body(): gathered = lax.all_gather(own_queries, 'blk', axis=0, tiled=True)  49.4 us
    all_to_all x1, waiting for transfers between devices, body(): lax.all_to_all(packed, 'blk', split_axis=0, concat_axis=0, tiled=True)  25.7 us
    unnamed x23, local copies, waits for them, and re-layouts  14.4 us
    all_to_all x1, starting transfers between devices, body(): lax.all_to_all(packed, 'blk', split_axis=0, concat_axis=0, tiled=True)  10 us
  transfers between devices with their start and end apart: 3, of which 3 were waited for; matrix products, arithmetic and copies ran while one was open for 7% of the time, Pallas kernels for 0%

commit v1 on v0

--- a/solution.py
+++ b/solution.py
@@ -78,7 +78,11 @@
         .reshape(FLAG_DEV, heads_dev, 2 * head_dim)
     )
     own_queries = projected[:, :, :head_dim].reshape(row_count, heads_dev * head_dim)
-    gathered = lax.all_gather(own_queries, "blk", axis=0, tiled=True)
+    length = lax.axis_size("blk")
+    repeats = [length if d == 0 else 1 for d in range(own_queries.ndim)]
+    gathered = lax.all_to_all(
+        jnp.tile(own_queries, repeats), "blk", split_axis=0, concat_axis=0, tiled=True
+    )
     prefix_keys = kv_cache[0].at[flagged].set(recomputed[:, :, :head_dim])
     prefix_values = kv_cache[1].at[flagged].set(recomputed[:, :, head_dim:])
     keys_all = jnp.concatenate([prefix_keys, projected[:, :, head_dim : 2 * head_dim]], axis=0)

time: 289 us -> 274 us (0.948)
  the two profiles are of different devices: /device:TPU:8 before, /device:TPU:1 now
where the time goes in v1:
time: 274 us; the launch traced here: 273 us
  waiting for transfers between devices  142 us (52%)
  local copies, waits for them, and re-layouts  53.1 us (19%)
  starting transfers between devices  27.6 us (10%)
  other arithmetic  23.7 us (9%)
  between operations  13.6 us (5%)
  matrix products  13.2 us (5%)
    all_gather x1, waiting for transfers between devices, body(): fetched_all = lax.all_gather(packed_weights, 'blk', axis=0, tiled=True)  93.7 us
    all_to_all x1, waiting for transfers between devices, body(): lax.all_to_all(packed, 'blk', split_axis=0, concat_axis=0, tiled=True)  32.9 us
    unnamed x21, local copies, waits for them, and re-layouts  14.4 us
    all_to_all x1, waiting for transfers between devices, body(): lax.all_to_all(jnp.tile(own_queries, repeats), 'blk', split_axis=0, conca...  10.7 us
    all_to_all x1, starting transfers between devices, body(): lax.all_to_all(jnp.tile(own_queries, repeats), 'blk', split_axis=0, conca...  9.79 us
    all_to_all x1, starting transfers between devices, body(): lax.all_to_all(packed, 'blk', split_axis=0, concat_axis=0, tiled=True)  9.26 us
    all_to_all x1, starting transfers between devices, body(): lax.all_to_all(pieces, 'head', split_axis=0, concat_axis=0, tiled=True)  8.58 us
  transfers between devices with their start and end apart: 4, of which 4 were waited for; matrix products, arithmetic and copies ran while one was open for 10% of the time, Pallas kernels for 0%

profile of v1, /device:TPU:1, one launch (start us, length us, event | category | flops | bytes accessed | tf_op | source)
XLA Modules:
  0.0 272.9 jit_solution(16990334677357716392)
XLA Ops:
  16.2 3.2 %sort.17 = (s32[256]{0:T(256)}, s32[256]{0:T(256)S(1)}) sort(s32[256]{0:T(256)S(1)} %broadcast_subtract_fusion, s32[256]{0:T(256)S(1)} %iota.25), dimensions={0}, to_apply=%region_7.8 | sort | flops 2048 | bytes 4096 | tf_op jit(solution)/shard_map/jit(argsort)/sort | solution.py:51
  21.6 93.7 %all-gather.3.cloned.1.call-done = bf16[64,1,32768]{2,1,0:T(2,128)(2,1)} async-done(((bf16[1,1,32768]{2,1,0:T(2,128)(2,1)}), bf16[64,1,32768]{2,1,0:T(2,128)(2,1)}) %all-gather.3.cloned.1.call-update) | async-done | bytes 4194320 | tf_op jit(solution)/shard_map/all_gather | solution.py:57
  115.2 7.9 %copy.55 = bf16[64,1,32768]{2,0,1:T(8,128)(2,1)S(1)} copy(bf16[64,1,32768]{2,1,0:T(2,128)(2,1)} %all-gather.3.cloned.1.call-done) | data formatting | bytes 8388608
  123.2 1.9 copy-done.1
  125.1 1.9 slice.62
  127.0 4.9 %reshape_reshape.3 = bf16[2048,768]{1,0:T(8,128)(2,1)} reshape(bf16[64,24576]{1,0:T(8,128)(2,1)} %slice.62) | data formatting | bytes 6291456 | tf_op jit(solution)/shard_map/reshape;reshape | solution.py:65
  131.8 2.5 fusion.19
  135.3 9.8 %all-to-all-start = ((bf16[64,24,256]{2,1,0:T(8,128)(2,1)}), bf16[64,24,256]{2,1,0:T(8,128)(2,1)S(1)}, u32[]{:S(2)}, u32[]{:S(2)}) async-start(bf16[64,24,256]{2,1,0:T(8,128)(2,1)} %tile.9), calls=%async_computation | async-start | bytes 1572864 | tf_op jit(solution)/shard_map/all_to_all | solution.py:83
  146.1 4.8 %reshape.224 = bf16[2048,1,768]{2,0,1:T(8,128)(2,1)} reshape(bf16[64,24576]{1,0:T(8,128)(2,1)} %slice.62) | data formatting | bytes 6291456 | tf_op jit(solution)/shard_map/reshape | solution.py:59
  151.0 2.1 fusion.20
  155.6 10.7 %all-to-all-done = bf16[64,24,256]{2,1,0:T(8,128)(2,1)S(1)} async-done(((bf16[64,24,256]{2,1,0:T(8,128)(2,1)}), bf16[64,24,256]{2,1,0:T(8,128)(2,1)S(1)}, u32[]{:S(2)}, u32[]{:S(2)}) %all-to-all-start) | async-done | bytes 786464 | tf_op jit(solution)/shard_map/all_to_all | solution.py:83
  167.5 11.9 %while.17 = (s32[]{:T(128)}, f32[1536,256]{1,0:T(8,128)S(1)}, f32[1536,1]{0,1:T(1,128)}, f32[1536,1]{0,1:T(1,128)}, s32[1536]{0:T(1024)}, /*index=5*/s32[280]{0:...) while((s32[]{:T(128)}, f32[1536,256]{1,0:T(8,128)S(1)}, ...), condition=%wide.region_15.16_spmd, body=%wide.region_12.15_spmd.sunk | while | flops 149380608 | bytes 2841579 | solution.py:138
  179.4 1.9 copy.40
  181.3 1.9 copy.39
  183.2 2.2 pad_maximum_fusion
  185.4 4.3 %all_to_all.20 = f32[64,1,6192]{2,1,0:T(1,128)} reshape(f32[1536,258]{1,0:T(8,128)S(1)} %pad_maximum_fusion) | data formatting | bytes 3170304 | tf_op jit(solution)/shard_map/all_to_all | solution.py:143
  189.7 9.3 %all-to-all-start.1 = ((f32[64,1,6192]{2,1,0:T(1,128)}), f32[64,1,6192]{2,1,0:T(1,128)S(1)}, u32[]{:S(2)}, u32[]{:S(2)}) async-start(f32[64,1,6192]{2,1,0:T(1,128)} %all_to_all.20), calls=%async_computation.1 | async-start | bytes 3211264 | tf_op jit(solution)/shard_map/all_to_all | solution.py:143
  199.0 2.3 slice.72
  201.2 2.7 reshape.228
  203.9 32.9 %all-to-all-done.1 = f32[64,1,6192]{2,1,0:T(1,128)S(1)} async-done(((f32[64,1,6192]{2,1,0:T(1,128)}), f32[64,1,6192]{2,1,0:T(1,128)S(1)}, u32[]{:S(2)}, u32[]{:S(2)}) %all-to-all-start.1) | async-done | bytes 1585184 | tf_op jit(solution)/shard_map/all_to_all | solution.py:143
  236.9 5.4 %reduce.14 = f32[64,6192]{1,0:T(8,128)} reduce(f32[64,1,6192]{2,1,0:T(1,128)S(1)} %all-to-all-done.1, f32[]{:T(128)} %constant.108), dimensions={1}, to_apply=%all_to_all.18.reduce_sub_computation | reduce | bytes 3170308 | tf_op jit(solution)/shard_map/all_to_all | solution.py:143
  242.2 2.5 reshape.227
  251.9 8.6 %all-to-all-start.2 = ((bf16[8,24,256]{2,1,0:T(8,128)(2,1)}), bf16[8,24,256]{2,1,0:T(8,128)(2,1)S(1)}, u32[]{:S(2)}, u32[]{:S(2)}) async-start(bf16[8,24,256]{2,1,0:T(8,128)(2,1)} %bitcast.72), calls=%async_computation.2 | async-start | bytes 196608 | tf_op jit(solution)/shard_map/all_to_all | solution.py:161
  261.2 4.2 %all-to-all-done.2 = bf16[8,24,256]{2,1,0:T(8,128)(2,1)S(1)} async-done(((bf16[8,24,256]{2,1,0:T(8,128)(2,1)}), bf16[8,24,256]{2,1,0:T(8,128)(2,1)S(1)}, u32[]{:S(2)}, u32[]{:S(2)}) %all-to-all-start.2) | async-done | bytes 98336 | tf_op jit(solution)/shard_map/all_to_all | solution.py:161
  (89 shorter events, 37.8 us)
Async XLA Ops:
  6.5 138.6 %copy-start = (bf16[256,2048]{1,0:T(8,128)(2,1)S(1)}, bf16[256,2048]{1,0:T(8,128)(2,1)}, u32[]{:S(2)}) copy-start(bf16[256,2048]{1,0:T(8,128)(2,1)} %param.16) | copy-start | bytes 3145732
  6.5 108.7 %all-gather.3.cloned.1.call-start = ((), (), s32[]{:S(2)}) async-start(), calls=%async_computation.3 | async-start | bytes 8519680 | tf_op jit(solution)/shard_map/all_gather | solution.py:57
  11.5 1.5 copy-start.6
  123.1 1.9 copy-start.1
  127.0 4.9 %copy-start.3 = (bf16[24,2048]{1,0:T(8,128)(2,1)S(1)}, bf16[24,2048]{1,0:T(8,128)(2,1)}, u32[]{:S(2)}) copy-start(bf16[24,2048]{1,0:T(8,128)(2,1)} %param.15) | copy-start | bytes 294916
  127.0 4.9 %copy-start.7 = (f32[2048]{0:T(1024)S(1)}, f32[2048]{0:T(1024)}, u32[]{:S(2)}) copy-start(f32[2048]{0:T(1024)} %param.19) | copy-start | bytes 24580
  127.0 4.9 %copy-start.8 = (f32[2048]{0:T(1024)S(1)}, f32[2048]{0:T(1024)}, u32[]{:S(2)}) copy-start(f32[2048]{0:T(1024)} %param.18) | copy-start | bytes 24580
  134.3 11.8 %copy-start.4 = (bf16[2,256,1,256]{3,1,2,0:T(8,128)(2,1)S(1)}, bf16[2,256,1,256]{3,1,2,0:T(8,128)(2,1)}, u32[]{:S(2)}) copy-start(bf16[2,256,1,256]{3,1,2,0:T(8,128)(2,1)} %param.17) | copy-start | bytes 786436
  135.3 31.0 %all-to-all-start = ((bf16[64,24,256]{2,1,0:T(8,128)(2,1)}), bf16[64,24,256]{2,1,0:T(8,128)(2,1)S(1)}, u32[]{:S(2)}, u32[]{:S(2)}) async-start(bf16[64,24,256]{2,1,0:T(8,128)(2,1)} %tile.9), calls=%async_computation | async-start | bytes 1572864 | tf_op jit(solution)/shard_map/all_to_all | solution.py:83
  146.1 4.8 %slice-start = ((f32[1,768]{1,0:T(1,128)}), f32[1,512]{1,0:T(1,128)S(1)}, s32[]{:S(2)}) async-start(f32[1,768]{1,0:T(1,128)} %param.21), calls=%async_computation.4 | async-start | bytes 4096 | tf_op jit(solution)/shard_map/slice | solution.py:76
  167.5 3.1 %copy-start.5 = (s32[280]{0:T(512)S(1)}, s32[280]{0:T(512)}, u32[]{:S(2)}) copy-start(s32[280]{0:T(512)} %get-tuple-element.320) | copy-start | bytes 3364 | tf_op jit(solution)/shard_map/while
  171.5 3.1 %copy-start.5 = (s32[280]{0:T(512)S(1)}, s32[280]{0:T(512)}, u32[]{:S(2)}) copy-start(s32[280]{0:T(512)} %get-tuple-element.320) | copy-start | bytes 3364 | tf_op jit(solution)/shard_map/while
  175.4 3.1 %copy-start.5 = (s32[280]{0:T(512)S(1)}, s32[280]{0:T(512)}, u32[]{:S(2)}) copy-start(s32[280]{0:T(512)} %get-tuple-element.320) | copy-start | bytes 3364 | tf_op jit(solution)/shard_map/while
  179.4 3.8 %copy-start.2 = (f32[1536,256]{1,0:T(8,128)}, f32[1536,256]{1,0:T(8,128)S(1)}, u32[]{:S(2)}) copy-start(f32[1536,256]{1,0:T(8,128)S(1)} %get-tuple-element.178) | copy-start | bytes 4718596
  189.7 47.2 %all-to-all-start.1 = ((f32[64,1,6192]{2,1,0:T(1,128)}), f32[64,1,6192]{2,1,0:T(1,128)S(1)}, u32[]{:S(2)}, u32[]{:S(2)}) async-start(f32[64,1,6192]{2,1,0:T(1,128)} %all_to_all.20), calls=%async_computation.1 | async-start | bytes 3211264 | tf_op jit(solution)/shard_map/all_to_all | solution.py:143
  251.9 13.6 %all-to-all-start.2 = ((bf16[8,24,256]{2,1,0:T(8,128)(2,1)}), bf16[8,24,256]{2,1,0:T(8,128)(2,1)S(1)}, u32[]{:S(2)}, u32[]{:S(2)}) async-start(bf16[8,24,256]{2,1,0:T(8,128)(2,1)} %bitcast.72), calls=%async_computation.2 | async-start | bytes 196608 | tf_op jit(solution)/shard_map/all_to_all | solution.py:161
Sparse Core Ops, SparseCore 0:
  10.4 104.8 all-gather.2
